TPU v7x, 512 devices: a whole 4x8x8 slice. The times are simulated.
512 devices in a mesh: shard: 128 (over y, z, core), tensor: 4 (over x).
Axes of the slice: x: 4, y: 8, z: 8, core: 2. Of those that a mesh axis runs over, the one named last changes fastest.
Arguments:
- grad_query: bfloat16 [128, 1024, 512], P('shard', None, 'tensor'), may hold values from -8 to 8
- error_query: float32 [128, 1024, 512], P('shard', None, 'tensor'), may hold values from -3 to 3
- grad_output: bfloat16 [128, 512, 1024], P('shard', 'tensor'), may hold values from -8 to 8
- error_output: float32 [128, 512, 1024], P('shard', 'tensor'), may hold values from -3 to 3
- start_query: float32 [512, 32], P('tensor'), may hold values from -6 to 6
- start_output: float32 [1024, 32], replicated, may hold values from -6 to 6
- weight_query: float32 [1024, 512], P('shard', 'tensor'), may hold values from -0.1875 to 0.1875
- weight_output: float32 [512, 1024], P('tensor', 'shard'), may hold values from -0.25 to 0.25
- moment_query: float32 [1024, 512], P('shard', 'tensor'), may hold values from -1.2 to 1.2
- moment_output: float32 [512, 1024], P('tensor', 'shard'), may hold values from -1.2 to 1.2
- grad_vector: bfloat16 [128, 3584], P('shard'), may hold values from -12 to 12
- moment_vector: float32 [3584], P('shard'), may hold values from -1.2 to 1.2
- weight_vector: float32 [3584], P('shard'), may hold values from 0.5 to 1.5
Outputs:
- new_error_query: float32 [128, 1024, 512], P('shard', None, 'tensor')
- new_error_output: float32 [128, 512, 1024], P('shard', 'tensor')
- new_moment_query: float32 [1024, 512], P('shard', 'tensor')
- new_moment_output: float32 [512, 1024], P('tensor', 'shard')
- new_weight_query: float32 [1024, 512], P(None, 'tensor')
- new_weight_output: float32 [512, 1024], P('tensor')
- new_moment_vector: float32 [3584], P('shard')
- new_weight_vector: float32 [3584], replicated
All inputs are finite; a program needn't handle non-finite values.
Results may differ from a plain program's by a relative error of at most 0.0003.
Values sent between devices are 32-bit elements; how exact they have to be, the bound alone decides.
No kernel may reach another device: no remote copies, remote signals or barrier semaphores. Data moves between devices by JAX's collectives and lax.ppermute only.
A program may use at most 64 MiB of HBM per device.

v0:
```python
import jax
import jax.numpy as jnp
from jax import lax
from jax.sharding import PartitionSpec as P

ROUNDS = 2
highest = lax.Precision.HIGHEST


def product(left, right):
    return jnp.dot(left, right, precision=highest, preferred_element_type=jnp.float32)


def product_inner(left, right):
    return lax.dot_general(
        left, right, (((0,), (0,)), ((), ())), precision=highest, preferred_element_type=jnp.float32
    )


def solve_rows(gram, factor):
    lower = jnp.linalg.cholesky(gram)
    return jax.scipy.linalg.solve_triangular(lower, factor.T, lower=True).T


def orthonormal(factor):
    return solve_rows(product_inner(factor, factor), factor)


def orthonormal_rows(factor):
    gram = lax.psum(product_inner(factor, factor), "tensor")
    return solve_rows(gram, factor)


def local(
    grad_query,
    error_query,
    grad_output,
    error_output,
    start_query,
    start_output,
    weight_query,
    weight_output,
    moment_query,
    moment_output,
    grad_vector,
    moment_vector,
    weight_vector,
):
    replicas = lax.axis_size("shard")
    shard_index = lax.axis_index("shard")
    total_query = grad_query[0].astype(jnp.float32) + error_query[0]
    total_output = grad_output[0].astype(jnp.float32) + error_output[0]
    factor_query = start_query
    factor_output = start_output
    for turn in range(ROUNDS):
        part_query = product(total_query, factor_query)
        part_output = product(total_output, factor_output)
        sum_query = lax.psum(part_query, ("shard", "tensor"))
        sum_output = lax.psum(part_output, "shard")
        left_query = orthonormal(sum_query)
        left_output = orthonormal_rows(sum_output)
        right_query_part = product_inner(total_query, left_query)
        right_output_part = product_inner(total_output, left_output)
        factor_query = lax.psum(right_query_part, "shard")
        factor_output = lax.psum(right_output_part, ("shard", "tensor"))
    approx_query = product(left_query, factor_query.T) / replicas
    approx_output = product(left_output, factor_output.T) / replicas
    new_error_query = (total_query - approx_query)[None]
    new_error_output = (total_output - approx_output)[None]
    rows_block = moment_query.shape[0]
    block_query = lax.dynamic_slice_in_dim(approx_query, shard_index * rows_block, rows_block, 0)
    cols_block = moment_output.shape[1]
    block_output = lax.dynamic_slice_in_dim(approx_output, shard_index * cols_block, cols_block, 1)
    new_moment_query = 0.9 * moment_query + block_query
    new_moment_output = 0.9 * moment_output + block_output
    stepped_query = weight_query - 0.01 * new_moment_query
    stepped_output = weight_output - 0.01 * new_moment_output
    local_vector = grad_vector[0].astype(jnp.float32)
    vector_block = moment_vector.shape[0]
    vector_whole = lax.psum(local_vector, "shard")
    vector_part = lax.dynamic_slice_in_dim(
        vector_whole, shard_index * vector_block, vector_block, 0
    )
    vector_mean = vector_part / replicas
    new_moment_vector = 0.9 * moment_vector + vector_mean
    stepped_vector = weight_vector - 0.01 * new_moment_vector
    new_weight_query, new_weight_output, new_weight_vector = (
        lax.all_gather(stepped_query, "shard", axis=0, tiled=True),
        lax.all_gather(stepped_output, "shard", axis=1, tiled=True),
        lax.all_gather(stepped_vector, "shard", axis=0, tiled=True),
    )
    return (
        new_error_query,
        new_error_output,
        new_moment_query,
        new_moment_output,
        new_weight_query,
        new_weight_output,
        new_moment_vector,
        new_weight_vector,
    )


def solution(mesh):
    in_specs = (
        P("shard", None, "tensor"),
        P("shard", None, "tensor"),
        P("shard", "tensor", None),
        P("shard", "tensor", None),
        P("tensor", None),
        P(),
        P("shard", "tensor"),
        P("tensor", "shard"),
        P("shard", "tensor"),
        P("tensor", "shard"),
        P("shard", None),
        P("shard"),
        P("shard"),
    )
    out_specs = (
        P("shard", None, "tensor"),
        P("shard", "tensor", None),
        P("shard", "tensor"),
        P("tensor", "shard"),
        P(None, "tensor"),
        P("tensor", None),
        P("shard"),
        P(),
    )
    return jax.shard_map(local, mesh=mesh, in_specs=in_specs, out_specs=out_specs, check_vma=False)
```

profile of v0, /device:TPU:1, one launch (start us, length us, event | category | flops | bytes accessed | tf_op | source)
XLA Modules:
  0.0 2203.4 jit_solution(7634404734054702130)
XLA Ops:
  9.1 498.1 %psum.81 = f32[128,32]{0,1:T(8,128)S(1)} all-reduce(f32[128,32]{0,1:T(8,128)S(1)} %fusion.6), channel_id=1, replica_groups=mesh['shard'=128,'tensor'=4] {'shard'}, use_global_device_ids=true, to_apply=%region_6.9 | all-reduce | flops 4096 | bytes 32768 | tf_op jit(solution)/shard_map/psum | solution.py:59
  507.3 13.2 psum.82
  520.6 2.9 cholesky.96
  524.9 2.4 custom-call.12
  527.6 1.3 fusion.4
  528.9 1.3 fusion.15
  530.3 1.3 dynamic-slice
  532.3 265.7 %all-reduce.10.cloned.1.call-done = (f32[1024,32]{0,1:T(8,128)}, f32[1024,32]{0,1:T(8,128)}) async-done(((f32[1024,32]{0,1:T(8,128)}, f32[1024,32]{0,1:T(8,128)}), (f32[1024,32]{0,1:T(8,128)}, f32[1024,32]{0,1:T(8,128)})) %all-reduce.10.cloned.1.call-update) | async-done | bytes 262160 | tf_op jit(solution)/shard_map/psum | solution.py:58
  798.0 1.4 fusion.2
  799.7 2.9 cholesky.74
  804.0 2.4 custom-call.10
  807.2 487.8 %all-reduce.4 = (f32[128,32]{0,1:T(8,128)S(1)}, f32[128,32]{0,1:T(8,128)S(1)}, f32[3584]{0:T(1024)S(1)}) all-reduce(f32[128,32]{0,1:T(8,128)S(1)} %fusion.13, f32[128,32]{0,1:T(8,128)S(1)} %fusion.2, f32[3584]{0:T(1024)S(1)} %convert_reduce_fusion), channel_id=1, replica_groups=mesh['shard'=128,'tensor'=4] {'shard'}, use_global_device_ids=true, to_apply=%region_3.6 | all-reduce | flops 11776 | bytes 94208 | tf_op jit(solution)/shard_map/psum | solution.py:64
  1295.2 12.4 psum.85
  1307.6 2.9 cholesky.107
  1311.9 2.4 custom-call.13
  1314.6 1.3 fusion.11
  1315.9 1.3 fusion
  1318.5 270.5 %all-reduce.8.cloned.1.call-done = (f32[1024,32]{0,1:T(8,128)}, f32[1024,32]{0,1:T(8,128)}) async-done(((f32[1024,32]{0,1:T(8,128)}, f32[1024,32]{0,1:T(8,128)}), (f32[1024,32]{0,1:T(8,128)}, f32[1024,32]{0,1:T(8,128)})) %all-reduce.8.cloned.1.call-update) | async-done | bytes 262160 | tf_op jit(solution)/shard_map/psum | solution.py:58
  1589.0 1.2 fusion.41
  1590.3 2.9 cholesky.85
  1594.6 2.4 custom-call.11
  1597.8 487.8 %all-reduce.3 = (f32[128,32]{0,1:T(8,128)S(1)}, f32[3584]{0:T(1024)}) all-reduce(f32[128,32]{0,1:T(8,128)S(1)} %fusion.9, f32[3584]{0:T(1024)S(1)} %get-tuple-element.48), channel_id=1, replica_groups=mesh['shard'=128,'tensor'=4] {'shard'}, use_global_device_ids=true, to_apply=%region_5.8 | all-reduce | flops 7680 | bytes 61440 | tf_op jit(solution)/shard_map/psum | solution.py:64
  2090.2 53.0 %all_gather.10 = f32[128,1024]{0,1:T(8,128)S(1)} all-gather(f32[128,8]{0,1:T(8,128)S(1)} %get-tuple-element.44), channel_id=1, replica_groups=mesh['shard'=128,'tensor'=4] {'shard'}, dimensions={1}, use_global_device_ids=true | all-gather | bytes 528384 | tf_op jit(solution)/shard_map/all_gather | solution.py:89
  2144.9 50.9 %all_gather.9 = f32[1024,128]{1,0:T(8,128)S(1)} all-gather(f32[8,128]{1,0:T(8,128)S(1)} %get-tuple-element.46), channel_id=1, replica_groups=mesh['shard'=128,'tensor'=4] {'shard'}, dimensions={0}, use_global_device_ids=true | all-gather | bytes 528384 | tf_op jit(solution)/shard_map/all_gather | solution.py:88
  (78 shorter events, 18.4 us)
Async XLA Ops:
  7.2 1.5 copy-start
  7.2 1.2 copy-start.5
  7.2 790.8 %all-reduce.10.cloned.1.call-start = ((), (), s32[]{:S(2)}) async-start(), calls=%async_computation.1 | async-start | bytes 524288 | tf_op jit(solution)/shard_map/psum | solution.py:58
  520.6 8.3 copy-start.1
  527.6 1.3 copy-start.2
  527.6 1.3 copy-start.7
  530.3 1058.7 %all-reduce.8.cloned.1.call-start = ((), (), s32[]{:S(2)}) async-start(), calls=%async_computation | async-start | bytes 524288 | tf_op jit(solution)/shard_map/psum | solution.py:58
  530.3 1.9 copy-start.8
  798.0 1.4 copy-start.3
  1317.2 0.7 copy-start.13
  1317.2 0.7 copy-start.14
  1590.2 6.8 copy-start.4
  2086.6 0.9 copy-start.6
  2088.6 1.0 copy-start.9
  2088.6 1.0 copy-start.10
  2143.3 1.0 copy-start.11
  2143.3 1.0 copy-start.12
Sparse Core Ops, SparseCore 0:
  530.4 267.5 all-reduce.9
  1317.3 271.6 all-reduce.7
where the time goes:
time: 2200 us
  blocking collectives  1600 us (73%)
  waiting for transfers between devices  536 us (24%)
  other arithmetic  29.5 us (1%)
    psum x2, blocking collectives, local(): factor_query = lax.psum(right_query_part, 'shard')  976 us
    psum x2, waiting for transfers between devices, local(): sum_query = lax.psum(part_query, ('shard', 'tensor'))  536 us
    psum x1, blocking collectives, local(): sum_output = lax.psum(part_output, 'shard')  498 us
    all_gather x1, blocking collectives, local(): lax.all_gather(stepped_output, 'shard', axis=1, tiled=True)  53 us
    all_gather x1, blocking collectives, local(): lax.all_gather(stepped_query, 'shard', axis=0, tiled=True)  50.9 us
  transfers between devices with their start and end apart: 2, of which 2 were waited for; matrix products, arithmetic and copies ran while one was open for 0% of the time, Pallas kernels for 0%

commit v1 on v0

--- a/solution.py
+++ b/solution.py
@@ -55,7 +55,7 @@
     for turn in range(ROUNDS):
         part_query = product(total_query, factor_query)
         part_output = product(total_output, factor_output)
-        sum_query = lax.psum(part_query, ("shard", "tensor"))
+        sum_query = lax.psum(lax.psum(part_query, "shard"), "tensor")
         sum_output = lax.psum(part_output, "shard")
         left_query = orthonormal(sum_query)
         left_output = orthonormal_rows(sum_output)

time: 2200 us -> 2100 us (0.955)
  blocking collectives: 1600 us -> 1110 us
  waiting for transfers between devices: 536 us -> 923 us
    psum x1 -> x0, blocking collectives: 498 us -> none  [local(): sum_output = lax.psum(part_output, 'shard')]
    psum x2 -> x6, waiting for transfers between devices: 536 us -> 923 us  [the longest x2 466 us: local(): factor_output = lax.psum(right_output_part, ('shard', 'tensor'))]
  transfers between devices with their start and end apart: 2 -> 6, of which waited for: 2 -> 6; matrix products, arithmetic and copies ran while one was open for 0% -> 0% of each run, Pallas kernels for 0% -> 0%
where the time goes in v1:
time: 2100 us
  blocking collectives  1110 us (53%)
  waiting for transfers between devices  923 us (44%)
  other arithmetic  29.5 us (1%)
    psum x2, blocking collectives, local(): factor_query = lax.psum(right_query_part, 'shard')  983 us
    psum x2, waiting for transfers between devices, local(): factor_output = lax.psum(right_output_part, ('shard', 'tensor'))  466 us
    psum x4, waiting for transfers between devices, local(): sum_query = lax.psum(lax.psum(part_query, 'shard'), 'tensor')  457 us
    all_gather x1, blocking collectives, local(): lax.all_gather(stepped_query, 'shard', axis=0, tiled=True)  55.5 us
    all_gather x1, blocking collectives, local(): lax.all_gather(stepped_output, 'shard', axis=1, tiled=True)  49 us
  transfers between devices with their start and end apart: 6, of which 6 were waited for; matrix products, arithmetic and copies ran while one was open for 0% of the time, Pallas kernels for 0%

profile of v1, /device:TPU:1, one launch (start us, length us, event | category | flops | bytes accessed | tf_op | source)
XLA Modules:
  0.0 2103.3 jit_solution(4282501225335525313)
XLA Ops:
  7.2 2.5 fusion.15
  11.0 189.1 %all-reduce.10.cloned.1.call-done = f32[1024,32]{0,1:T(8,128)} async-done(((f32[1024,32]{0,1:T(8,128)}), f32[1024,32]{0,1:T(8,128)}) %all-reduce.10.cloned.1.call-update) | async-done | bytes 131088 | tf_op jit(solution)/shard_map/psum | solution.py:58
  200.6 1.3 dynamic-slice
  202.6 43.5 %all-reduce.12.cloned.1.call-done = f32[1024,32]{0,1:T(8,128)} async-done(((f32[1024,32]{0,1:T(8,128)}), f32[1024,32]{0,1:T(8,128)}) %all-reduce.12.cloned.1.call-update) | async-done | bytes 131088 | tf_op jit(solution)/shard_map/psum | solution.py:58
  247.5 2.9 cholesky.74
  251.7 2.4 custom-call.10
  255.9 491.5 %all-reduce.2 = (f32[128,32]{0,1:T(8,128)S(1)}, f32[128,32]{0,1:T(8,128)S(1)}, f32[3584]{0:T(1024)S(1)}) all-reduce(f32[128,32]{0,1:T(8,128)S(1)} %fusion.13, f32[128,32]{0,1:T(8,128)S(1)} %fusion.6, f32[3584]{0:T(1024)S(1)} %convert_reduce_fusion), channel_id=1, replica_groups=mesh['shard'=128,'tensor'=4] {'shard'}, use_global_device_ids=true, to_apply=%region_4.7 | all-reduce | flops 11776 | bytes 94208 | tf_op jit(solution)/shard_map/psum | solution.py:64
  747.6 12.3 psum.98
  759.9 2.9 cholesky.96
  764.2 2.4 custom-call.12
  770.9 180.2 %all-reduce.14.cloned.1.call-done = f32[1024,32]{0,1:T(8,128)} async-done(((f32[1024,32]{0,1:T(8,128)}), f32[1024,32]{0,1:T(8,128)}) %all-reduce.14.cloned.1.call-update) | async-done | bytes 131088 | tf_op jit(solution)/shard_map/psum | solution.py:58
  951.1 261.9 %all-reduce.18.cloned.1.call-done = f32[1024,32]{0,1:T(8,128)} async-done(((f32[1024,32]{0,1:T(8,128)}), f32[1024,32]{0,1:T(8,128)}) %all-reduce.18.cloned.1.call-update) | async-done | bytes 131088 | tf_op jit(solution)/shard_map/psum | solution.py:65
  1213.0 1.3 fusion.2
  1214.4 44.0 %all-reduce.16.cloned.1.call-done = f32[1024,32]{0,1:T(8,128)} async-done(((f32[1024,32]{0,1:T(8,128)}), f32[1024,32]{0,1:T(8,128)}) %all-reduce.16.cloned.1.call-update) | async-done | bytes 131088 | tf_op jit(solution)/shard_map/psum | solution.py:58
  1259.7 2.9 cholesky.85
  1264.0 2.4 custom-call.11
  1267.2 491.5 %all-reduce.1 = (f32[128,32]{0,1:T(8,128)S(1)}, f32[128,32]{0,1:T(8,128)S(1)}, f32[3584]{0:T(1024)}) all-reduce(f32[128,32]{0,1:T(8,128)S(1)} %fusion.9, f32[128,32]{0,1:T(8,128)S(1)} %fusion.2, f32[3584]{0:T(1024)S(1)} %get-tuple-element.45), channel_id=1, replica_groups=mesh['shard'=128,'tensor'=4] {'shard'}, use_global_device_ids=true, to_apply=%region_7.10 | all-reduce | flops 11776 | bytes 94208 | tf_op jit(solution)/shard_map/psum | solution.py:64
  1758.9 12.3 psum.101
  1771.3 2.9 cholesky.107
  1775.5 2.4 custom-call.13
  1782.0 55.5 %all_gather.9 = f32[1024,128]{1,0:T(8,128)S(1)} all-gather(f32[8,128]{1,0:T(8,128)S(1)} %get-tuple-element.43), channel_id=1, replica_groups=mesh['shard'=128,'tensor'=4] {'shard'}, dimensions={0}, use_global_device_ids=true | all-gather | bytes 528384 | tf_op jit(solution)/shard_map/all_gather | solution.py:88
  1837.5 204.5 %all-reduce.20.cloned.1.call-done = f32[1024,32]{0,1:T(8,128)} async-done(((f32[1024,32]{0,1:T(8,128)}), f32[1024,32]{0,1:T(8,128)}) %all-reduce.20.cloned.1.call-update) | async-done | bytes 131088 | tf_op jit(solution)/shard_map/psum | solution.py:65
  2042.0 1.9 convolution_multiply_fusion
  2045.6 49.0 %all_gather.10 = f32[128,1024]{0,1:T(8,128)S(1)} all-gather(f32[128,8]{0,1:T(8,128)S(1)} %get-tuple-element.41), channel_id=1, replica_groups=mesh['shard'=128,'tensor'=4] {'shard'}, dimensions={1}, use_global_device_ids=true | all-gather | bytes 528384 | tf_op jit(solution)/shard_map/all_gather | solution.py:89
  (85 shorter events, 24.4 us)
Async XLA Ops:
  7.2 192.9 %copy-start = (f32[1024,32]{0,1:T(8,128)S(1)}, f32[1024,32]{0,1:T(8,128)}, u32[]{:S(2)}) copy-start(f32[1024,32]{0,1:T(8,128)} %param.23) | copy-start | bytes 393220
  7.2 192.8 %all-reduce.10.cloned.1.call-start = ((), (), s32[]{:S(2)}) async-start(), calls=%async_computation | async-start | bytes 262144 | tf_op jit(solution)/shard_map/psum | solution.py:58
  7.2 2.6 copy-start.5
  9.7 1.0 copy-start.4
  9.7 236.4 %all-reduce.12.cloned.1.call-start = ((), (), s32[]{:S(2)}) async-start(), calls=%async_computation.1 | async-start | bytes 262144 | tf_op jit(solution)/shard_map/psum | solution.py:58
  200.1 751.0 %all-reduce.14.cloned.1.call-start = ((), (), s32[]{:S(2)}) async-start(), calls=%async_computation.2 | async-start | bytes 262144 | tf_op jit(solution)/shard_map/psum | solution.py:58
  200.1 2.5 copy-start.6
  200.1 55.3 %copy-start.2 = (bf16[1,1024,128]{2,1,0:T(8,128)(2,1)S(1)}, bf16[1,1024,128]{2,1,0:T(8,128)(2,1)}, u32[]{:S(2)}) copy-start(bf16[1,1024,128]{2,1,0:T(8,128)(2,1)} %param.18) | copy-start | bytes 786436
  200.6 54.8 %copy-start.1 = (f32[1,1024,128]{2,1,0:T(8,128)S(1)}, f32[1,1024,128]{2,1,0:T(8,128)}, u32[]{:S(2)}) copy-start(f32[1,1024,128]{2,1,0:T(8,128)} %param.19) | copy-start | bytes 1572868
  768.2 444.9 %all-reduce.18.cloned.1.call-start = ((), (), s32[]{:S(2)}) async-start(), calls=%async_computation.4 | async-start | bytes 262144 | tf_op jit(solution)/shard_map/psum | solution.py:65
  769.6 488.8 %all-reduce.16.cloned.1.call-start = ((), (), s32[]{:S(2)}) async-start(), calls=%async_computation.3 | async-start | bytes 262144 | tf_op jit(solution)/shard_map/psum | solution.py:58
  769.6 0.7 copy-start.11
  769.6 0.7 copy-start.12
  951.1 1090.9 %all-reduce.20.cloned.1.call-start = ((), (), s32[]{:S(2)}) async-start(), calls=%async_computation.5 | async-start | bytes 262144 | tf_op jit(solution)/shard_map/psum | solution.py:65
  1259.6 6.8 copy-start.3
  1780.5 0.9 copy-start.7
  1780.6 0.9 copy-start.8
  2044.0 1.0 copy-start.9
  2044.0 1.0 copy-start.10
Sparse Core Ops, SparseCore 0:
  11.9 188.1 all-reduce.9
  202.3 43.7 all-reduce.11
  768.3 182.7 all-reduce.13
  957.3 255.7 all-reduce.17
  1215.2 43.1 all-reduce.15
  1779.7 262.2 all-reduce.19
